TPU v7x, 128 devices: a whole 4x4x4 slice. The times are simulated.
128 devices in a mesh: pts: 4 (over x_lo, core), comp: 32 (over x_hi, y, z).
Axes of the slice: x: 4 (x_hi: 2, x_lo: 2; x = x_hi * 2 + x_lo), y: 4, z: 4, core: 2. Of those that a mesh axis runs over, the one named last changes fastest.
Arguments:
- points: bfloat16 [1536, 512], P(('pts', 'comp')), may hold values from -28 to 28
- centres: bfloat16 [2048, 512], P('comp'), may hold values from -5 to 5
- whitening: bfloat16 [2048, 512, 512], P('comp', 'pts'), as said below
- log_prior: float32 [2048], P('comp'), may hold values from -4 to 4
Outputs:
- counts: float32 [2048], P('comp')
- first_moments: float32 [2048, 512], P('comp')
- second_moments: float32 [2048, 512, 512], P('comp', 'pts')
Inputs may be any that keep to these rules, and one draw needn't show every extreme that they name: Each whitening[k] is lower triangular with diagonal entries between 0.69 and 2.82.
All inputs are finite; a program needn't handle non-finite values.
Results may differ from a plain program's by a relative error of at most 0.0029.
Values may be sent and summed in bfloat16 or wider, within the bound.
No kernel may reach another device: no remote copies, remote signals or barrier semaphores. Data moves between devices by JAX's collectives and lax.ppermute only.
A program may use at most 128 MiB of HBM per device.

v0:
```python
import jax
import jax.numpy as jnp
from jax import lax
from jax.sharding import PartitionSpec as P

D = 512
anneal_beta = 1.25


def normalise(partial_total, prior_col):
    logits = anneal_beta * (prior_col - partial_total / D)
    row_peak = lax.pmax(jnp.max(logits, axis=0), "comp")
    expo_vals = jnp.exp(logits - row_peak[None, :])
    row_total = lax.psum(jnp.sum(expo_vals, axis=0), "comp")
    return (expo_vals / row_total[None, :]).astype(jnp.bfloat16)


def body(points, centres, whitening, log_prior):
    gathered = lax.all_gather(points, ("pts", "comp"), axis=0, tiled=True)
    comp_here = whitening.shape[0]
    band_rows = whitening.shape[1]
    total_points = gathered.shape[0]
    band_start = lax.axis_index("pts") * band_rows
    block_count = comp_here // 8
    factor_blocks = whitening.reshape(block_count, 8, band_rows, D)
    centre_blocks = centres.reshape(block_count, 8, D)

    def block_term(pair):
        factor, centre = pair
        offset = jnp.einsum("kqd,kd->kq", factor, centre, preferred_element_type=jnp.float32)
        whitened = (
            jnp.einsum("kqd,nd->kqn", factor, gathered, preferred_element_type=jnp.float32)
            - offset[:, :, None]
        )
        square_cols = lax.dynamic_slice_in_dim(factor, band_start, band_rows, 2)
        diag_vals = jnp.diagonal(square_cols, axis1=1, axis2=2).astype(jnp.float32)
        return (
            0.5 * jnp.sum(whitened * whitened, axis=1)
            - jnp.sum(jnp.log(diag_vals), axis=1)[:, None]
        )

    partial_term = lax.map(block_term, (factor_blocks, centre_blocks)).reshape(
        comp_here, total_points
    )
    prior_col = log_prior[:, None]
    summed = lax.psum(partial_term, "pts")
    responsibility = normalise(summed, prior_col)
    counts = jnp.sum(responsibility.astype(jnp.float32), axis=1)
    first_moments = jnp.dot(responsibility, gathered, preferred_element_type=jnp.float32)
    band_points = lax.dynamic_slice_in_dim(gathered, band_start, band_rows, 1).T.astype(jnp.float32)

    def block_second(resp_block):
        weighted = (resp_block.astype(jnp.float32)[:, None, :] * band_points[None, :, :]).astype(
            jnp.bfloat16
        )
        return jnp.einsum("kqn,nd->kqd", weighted, gathered, preferred_element_type=jnp.float32)

    second_moments = lax.map(block_second, responsibility.reshape(block_count, 8, total_points))
    return (counts, first_moments, second_moments.reshape(comp_here, band_rows, D))


def solution(mesh):
    in_specs = (P(("pts", "comp"), None), P("comp", None), P("comp", "pts", None), P("comp"))
    out_specs = (P("comp"), P("comp", None), P("comp", "pts", None))
    return jax.shard_map(body, mesh=mesh, in_specs=in_specs, out_specs=out_specs, check_vma=False)
```

profile of v0, /device:TPU:0, one launch (start us, length us, event | category | flops | bytes accessed | tf_op | source)
XLA Modules:
  0.0 677.8 jit_solution(2913701126033206041)
XLA Ops:
  8.0 305.8 %all-gather.3.cloned.1.call-done = bf16[128,12,512]{2,1,0:T(8,128)(2,1)} async-done(((bf16[1,12,512]{2,1,0:T(8,128)(2,1)}), bf16[128,12,512]{2,1,0:T(8,128)(2,1)}) %all-gather.3.cloned.1.call-update) | async-done | bytes 1572880 | tf_op jit(solution)/shard_map/all_gather | solution.py:19
  313.8 2.5 reshape.85
  316.3 99.1 %while.23 = (s32[]{:T(128)}, f32[8,8,1536]{2,1,0:T(8,128)}, bf16[8,8,128,512]{3,2,1,0:T(8,128)(2,1)}, bf16[1536,512]{1,0:T(8,128)(2,1)S(1)}, bf16[8,8,512]{2,1,0...) while((s32[]{:T(128)}, f32[8,8,1536]{2,1,0:T(8,128)}, bf16[8,8,128,512]{3,2,1,0:T(8,128)(2,1)}, ...), condition=%wide.region_3.4_spmd, body=%wide.region_0.3_spmd.sunk | while | flops 1616394752 | bytes 4908217 | solution.py:42
  318.6 3.1 multiply_reduce_fusion.2
  322.9 3.1 copy.20
  331.0 3.1 multiply_reduce_fusion.2
  335.3 3.1 copy.20
  338.3 2.0 gather_fusion
  343.3 3.1 multiply_reduce_fusion.2
  347.6 3.1 copy.20
  355.7 3.1 multiply_reduce_fusion.2
  360.0 3.1 copy.20
  368.1 3.1 multiply_reduce_fusion.2
  372.4 3.1 copy.20
  380.5 3.1 multiply_reduce_fusion.2
  384.8 3.1 copy.20
  392.9 3.1 multiply_reduce_fusion.2
  397.2 3.1 copy.20
  405.3 3.1 multiply_reduce_fusion.2
  409.5 3.1 copy.20
  415.7 38.1 %all-reduce.2.cloned.1.call-done = f32[64,1536]{1,0:T(8,128)} async-done(((f32[64,1536]{1,0:T(8,128)}), f32[64,1536]{1,0:T(8,128)}) %all-reduce.2.cloned.1.call-update) | async-done | bytes 393232 | tf_op jit(solution)/shard_map/psum | solution.py:46
  455.0 97.2 %pmax.7 = f32[1536]{0:T(1024)S(1)} all-reduce(f32[1536]{0:T(1024)S(1)} %fusion.15), channel_id=1, replica_groups=mesh['pts'=4,'comp'=32] {'comp'}, use_global_device_ids=true, to_apply=%region_6.7 | all-reduce | flops 1536 | bytes 12288 | tf_op jit(solution)/shard_map/pmax | solution.py:12
  553.3 90.0 %psum.15 = f32[1536]{0:T(1024)S(1)} all-reduce(f32[1536]{0:T(1024)S(1)} %fusion.14), channel_id=1, replica_groups=mesh['pts'=4,'comp'=32] {'comp'}, use_global_device_ids=true, to_apply=%region_8.9 | all-reduce | flops 1536 | bytes 12288 | tf_op jit(solution)/shard_map/psum | solution.py:14
  646.1 24.9 %while.24 = (s32[]{:T(128)}, f32[8,8,128,512]{3,2,1,0:T(8,128)}, bf16[8,8,1536]{2,1,0:T(8,128)(2,1)S(1)}, f32[128,1536]{1,0:T(8,128)S(1)}, bf16[1536,512]{1,0:T(8,128)(2,1)S(1)}, /*index=5*/s32[]{:T(128)}) while((s32[]{:T(128)}, f32[8,8,128,512]{3,2,1,0:T(8,128)}, bf16[8,8,1536]{2,1,0:T(8,128)(2,1)S(1)}, f32[128,1536]{1,0:T(8,128)S(1)}, ...), condition=%wide.region_11.12_spmd, body=%wide.region_10.11_spmd.sunk | while | flops 1613770752 | bytes 4579913 | solution.py:58
  646.1 3.1 bitcast_dynamic-update-slice_fusion.2
  649.2 3.1 bitcast_dynamic-update-slice_fusion.2
  652.4 3.1 bitcast_dynamic-update-slice_fusion.2
  655.5 3.1 bitcast_dynamic-update-slice_fusion.2
  658.6 3.1 bitcast_dynamic-update-slice_fusion.2
  661.7 3.1 bitcast_dynamic-update-slice_fusion.2
  664.8 3.1 bitcast_dynamic-update-slice_fusion.2
  667.9 3.1 bitcast_dynamic-update-slice_fusion.2
  (77 shorter events, 53.9 us)
Async XLA Ops:
  7.2 306.6 %all-gather.3.cloned.1.call-start = ((), (), s32[]{:S(2)}) async-start(), calls=%async_computation.1 | async-start | bytes 2113536 | tf_op jit(solution)/shard_map/all_gather | solution.py:19
  7.9 446.0 %all-reduce.2.cloned.1.call-start = ((), (), s32[]{:S(2)}) async-start(), calls=%async_computation | async-start | bytes 786432 | tf_op jit(solution)/shard_map/psum | solution.py:46
  316.3 137.6 %copy-start = (f32[64]{0:T(128)S(1)}, f32[64]{0:T(128)}, u32[]{:S(2)}) copy-start(f32[64]{0:T(128)} %param.11) | copy-start | bytes 772
Sparse Core Ops, SparseCore 0:
  9.7 304.0 all-gather.2
  415.5 38.3 all-reduce.1
where the time goes:
time: 680 us; the launch traced here: 678 us
  waiting for transfers between devices  345 us (51%)
  blocking collectives  187 us (28%)
  matrix products  63.2 us (9%)
  local copies, waits for them, and re-layouts  58.3 us (9%)
  between operations  14.1 us (2%)
  other arithmetic  10.1 us (1%)
    all_gather x1, waiting for transfers between devices, body(): gathered = lax.all_gather(points, ('pts', 'comp'), axis=0, tiled=True)  306 us
    pmax x1, blocking collectives, normalise(): row_peak = lax.pmax(jnp.max(logits, axis=0), 'comp')  97.2 us
    psum x1, blocking collectives, normalise(): row_total = lax.psum(jnp.sum(expo_vals, axis=0), 'comp')  90 us
    psum x1, waiting for transfers between devices, body(): summed = lax.psum(partial_term, 'pts')  38.1 us
    dynamic_slice x16, local copies, waits for them, and re-layouts, block_term(): square_cols = lax.dynamic_slice_in_dim(factor, band_start, band_rows, 2)  34.1 us
    dot_general x8, matrix products, block_second(): jnp.einsum('kqn,nd->kqd', weighted, gathered, preferred_element_type=jnp....  24.8 us
    dot_general x8, matrix products, block_term(): jnp.einsum('kqd,nd->kqn', factor, gathered, preferred_element_type=jnp.fl...  24.7 us
    gather x8, local copies, waits for them, and re-layouts, block_term(): diag_vals = jnp.diagonal(square_cols, axis1=1, axis2=2).astype(jnp.float32)  15.9 us
  transfers between devices with their start and end apart: 2, of which 2 were waited for; matrix products, arithmetic and copies ran while one was open for 0% of the time, Pallas kernels for 0%

commit v1 on v0

--- a/solution.py
+++ b/solution.py
@@ -16,7 +16,10 @@
 
 
 def body(points, centres, whitening, log_prior):
-    gathered = lax.all_gather(points, ("pts", "comp"), axis=0, tiled=True)
+    gathered = jnp.concatenate(
+        lax.all_to_all(jnp.stack([points] * lax.axis_size(("pts", "comp"))), ("pts", "comp"), 0, 0),
+        axis=0,
+    )
     comp_here = whitening.shape[0]
     band_rows = whitening.shape[1]
     total_points = gathered.shape[0]

time: 680 us -> 415 us (0.61)
  waiting for transfers between devices: 345 us -> 61.6 us
  starting transfers between devices: 0.08 us -> 11.2 us
    all_gather x1 -> x0, waiting for transfers between devices: 306 us -> none  [body(): gathered = lax.all_gather(points, ('pts', 'comp'), axis=0, tiled=True)]
    all_to_all x0 -> x1, waiting for transfers between devices: none -> 28.7 us  [body(): lax.all_to_all(jnp.stack([points] * lax.axis_size(('pts', 'comp'))), ('pt...]
    all_to_all x0 -> x1, starting transfers between devices: none -> 11.2 us  [body(): lax.all_to_all(jnp.stack([points] * lax.axis_size(('pts', 'comp'))), ('pt...]
where the time goes in v1:
time: 415 us; the launch traced here: 414 us
  blocking collectives  187 us (45%)
  matrix products  68.7 us (17%)
  waiting for transfers between devices  61.6 us (15%)
  local copies, waits for them, and re-layouts  59.5 us (14%)
  between operations  14.1 us (3%)
  starting transfers between devices  11.2 us (3%)
  other arithmetic  11.2 us (3%)
    pmax x1, blocking collectives, normalise(): row_peak = lax.pmax(jnp.max(logits, axis=0), 'comp')  97.2 us
    psum x1, blocking collectives, normalise(): row_total = lax.psum(jnp.sum(expo_vals, axis=0), 'comp')  90 us
    dynamic_slice x16, local copies, waits for them, and re-layouts, block_term(): square_cols = lax.dynamic_slice_in_dim(factor, band_start, band_rows, 2)  34.1 us
    psum x1, waiting for transfers between devices, body(): summed = lax.psum(partial_term, 'pts')  32.8 us
    all_to_all x1, waiting for transfers between devices, body(): lax.all_to_all(jnp.stack([points] * lax.axis_size(('pts', 'comp'))), ('pt...  28.7 us
    dot_general x8, matrix products, block_term(): jnp.einsum('kqd,nd->kqn', factor, gathered, preferred_element_type=jnp.fl...  28.7 us
    dot_general x8, matrix products, block_second(): jnp.einsum('kqn,nd->kqd', weighted, gathered, preferred_element_type=jnp....  24.8 us
    gather x8, local copies, waits for them, and re-layouts, block_term(): diag_vals = jnp.diagonal(square_cols, axis1=1, axis2=2).astype(jnp.float32)  15.9 us
  transfers between devices with their start and end apart: 2, of which 2 were waited for; matrix products, arithmetic and copies ran while one was open for 0% of the time, Pallas kernels for 0%

profile of v1, /device:TPU:0, one launch (start us, length us, event | category | flops | bytes accessed | tf_op | source)
XLA Modules:
  0.0 413.6 jit_solution(5923604404470989325)
XLA Ops:
  9.5 11.2 %all-to-all-start = ((bf16[128,12,512]{2,1,0:T(8,128)(2,1)}), bf16[128,12,512]{2,1,0:T(8,128)(2,1)S(1)}, u32[]{:S(2)}, u32[]{:S(2)}) async-start(bf16[128,12,512]{2,1,0:T(8,128)(2,1)} %stack.2), calls=%async_computation | async-start | bytes 4194304 | tf_op jit(solution)/shard_map/all_to_all | solution.py:20
  20.7 28.7 %all-to-all-done = bf16[128,12,512]{2,1,0:T(8,128)(2,1)S(1)} async-done(((bf16[128,12,512]{2,1,0:T(8,128)(2,1)}), bf16[128,12,512]{2,1,0:T(8,128)(2,1)S(1)}, u32[]{:S(2)}, u32[]{:S(2)}) %all-to-all-start) | async-done | bytes 1572896 | tf_op jit(solution)/shard_map/all_to_all | solution.py:20
  50.8 103.1 %while.23 = (s32[]{:T(128)}, f32[8,8,1536]{2,1,0:T(8,128)}, bf16[8,8,128,512]{3,2,1,0:T(8,128)(2,1)}, bf16[1536,512]{1,0:T(8,128)(2,1)}, bf16[8,8,512]{2,1,0:T(8...) while((s32[]{:T(128)}, f32[8,8,1536]{2,1,0:T(8,128)}, bf16[8,8,128,512]{3,2,1,0:T(8,128)(2,1)}, ...), condition=%wide.region_3.4_spmd, body=%wide.region_0.3_spmd.sunk | while | flops 1616394752 | bytes 4908217 | solution.py:45
  53.1 3.6 multiply_reduce_fusion.2
  57.9 3.1 copy.18
  66.0 3.6 multiply_reduce_fusion.2
  70.8 3.1 copy.18
  78.8 3.6 multiply_reduce_fusion.2
  83.6 3.1 copy.18
  91.7 3.6 multiply_reduce_fusion.2
  96.5 3.1 copy.18
  104.6 3.6 multiply_reduce_fusion.2
  109.4 3.1 copy.18
  117.5 3.6 multiply_reduce_fusion.2
  122.3 3.1 copy.18
  130.4 3.6 multiply_reduce_fusion.2
  135.2 3.1 copy.18
  143.3 3.6 multiply_reduce_fusion.2
  148.1 3.1 copy.18
  155.4 32.8 %all-reduce.2.cloned.1.call-done = f32[64,1536]{1,0:T(8,128)} async-done(((f32[64,1536]{1,0:T(8,128)}), f32[64,1536]{1,0:T(8,128)}) %all-reduce.2.cloned.1.call-update) | async-done | bytes 393232 | tf_op jit(solution)/shard_map/psum | solution.py:49
  189.3 97.2 %pmax.7 = f32[1536]{0:T(1024)S(1)} all-reduce(f32[1536]{0:T(1024)S(1)} %fusion.15), channel_id=1, replica_groups=mesh['pts'=4,'comp'=32] {'comp'}, use_global_device_ids=true, to_apply=%region_6.7 | all-reduce | flops 1536 | bytes 12288 | tf_op jit(solution)/shard_map/pmax | solution.py:12
  287.7 90.0 %psum.15 = f32[1536]{0:T(1024)S(1)} all-reduce(f32[1536]{0:T(1024)S(1)} %fusion.14), channel_id=1, replica_groups=mesh['pts'=4,'comp'=32] {'comp'}, use_global_device_ids=true, to_apply=%region_8.9 | all-reduce | flops 1536 | bytes 12288 | tf_op jit(solution)/shard_map/psum | solution.py:14
  379.4 2.4 fusion.16
  381.9 24.9 %while.24 = (s32[]{:T(128)}, f32[8,8,128,512]{3,2,1,0:T(8,128)}, bf16[8,8,1536]{2,1,0:T(8,128)(2,1)S(1)}, f32[128,1536]{1,0:T(8,128)S(1)}, bf16[1536,512]{1,0:T(8,128)(2,1)S(1)}, /*index=5*/s32[]{:T(128)}) while((s32[]{:T(128)}, f32[8,8,128,512]{3,2,1,0:T(8,128)}, bf16[8,8,1536]{2,1,0:T(8,128)(2,1)S(1)}, f32[128,1536]{1,0:T(8,128)S(1)}, ...), condition=%wide.region_11.12_spmd, body=%wide.region_10.11_spmd.sunk | while | flops 1613770752 | bytes 4579913 | solution.py:61
  381.9 3.1 bitcast_dynamic-update-slice_fusion.2
  385.0 3.1 bitcast_dynamic-update-slice_fusion.2
  388.1 3.1 bitcast_dynamic-update-slice_fusion.2
  391.2 3.1 bitcast_dynamic-update-slice_fusion.2
  394.3 3.1 bitcast_dynamic-update-slice_fusion.2
  397.4 3.1 bitcast_dynamic-update-slice_fusion.2
  400.5 3.1 bitcast_dynamic-update-slice_fusion.2
  403.6 3.1 bitcast_dynamic-update-slice_fusion.2
  (79 shorter events, 58.9 us)
Async XLA Ops:
  9.5 40.0 %all-to-all-start = ((bf16[128,12,512]{2,1,0:T(8,128)(2,1)}), bf16[128,12,512]{2,1,0:T(8,128)(2,1)S(1)}, u32[]{:S(2)}, u32[]{:S(2)}) async-start(bf16[128,12,512]{2,1,0:T(8,128)(2,1)} %stack.2), calls=%async_computation | async-start | bytes 4194304 | tf_op jit(solution)/shard_map/all_to_all | solution.py:20
  20.6 167.5 %all-reduce.2.cloned.1.call-start = ((), (), s32[]{:S(2)}) async-start(), calls=%async_computation.1 | async-start | bytes 786432 | tf_op jit(solution)/shard_map/psum | solution.py:49
  50.8 137.4 %copy-start.1 = (f32[64]{0:T(128)S(1)}, f32[64]{0:T(128)}, u32[]{:S(2)}) copy-start(f32[64]{0:T(128)} %param.11) | copy-start | bytes 772
  153.9 228.0 %copy-start = (bf16[1536,512]{1,0:T(8,128)(2,1)S(1)}, bf16[1536,512]{1,0:T(8,128)(2,1)}, u32[]{:S(2)}) copy-start(bf16[1536,512]{1,0:T(8,128)(2,1)} %get-tuple-element.294) | copy-start | bytes 4718596
Sparse Core Ops, SparseCore 0:
  154.0 34.1 all-reduce.1
